TPU v7x, 128 devices: a whole 4x4x4 slice. The times are simulated.
128 devices in a mesh: ctx: 128 (over x, y, z, core).
Axes of the slice: x: 4, y: 4, z: 4, core: 2. Of those that a mesh axis runs over, the one named last changes fastest.
Arguments:
- queries: bfloat16 [32768, 2048], P('ctx')
- keys: bfloat16 [32768, 512], P('ctx')
- values: bfloat16 [32768, 512], P('ctx'), may hold values from -6 to 6
- cotangent: bfloat16 [32768, 2048], P('ctx'), may hold values from -180 to 180
- summary_positions: int32 [256], replicated, may hold values from 0 to 32767, as said below
Outputs:
- query_grad: bfloat16 [32768, 2048], P('ctx')
- key_grad: bfloat16 [32768, 512], P('ctx')
- value_gradient: bfloat16 [32768, 512], P('ctx')
Inputs may be any that keep to these rules, and one draw needn't show every extreme that they name: `summary_positions`: entry m lies in [m * 128, (m + 1) * 128); the first entry is 0 and the last is 32767.
All inputs are finite; a program needn't handle non-finite values.
Results may differ from a plain program's by a relative error of at most 0.012.
The roundings to bfloat16 on the way count: a program that leaves them out, or rounds other values in their place, can miss the bound.
Values may be sent and summed in bfloat16 or wider, within the bound.
No kernel may reach another device: no remote copies, remote signals or barrier semaphores. Data moves between devices by JAX's collectives and lax.ppermute only.
A program may use at most 128 MiB of HBM per device.

v0:
```python
import jax
import jax.numpy as jnp
from jax import lax
from jax.sharding import PartitionSpec as P

HEAD = 128
BAND_LENGTH = 1024
NEGATIVE = -1e30


def passed_along(block, axis, distance):
    devices = range(lax.axis_size(axis))
    route = [(i - distance, i) for i in devices if i - distance in devices]
    return lax.ppermute(block, axis, route)


def group_pass(
    group_query, group_cot, band_keys, band_vals, summ_keys, summ_vals, band_mask, summ_mask, scale
):
    band_score = (
        jnp.einsum("tgd,kd->gtk", group_query, band_keys, preferred_element_type=jnp.float32)
        * scale
    )
    band_score = jnp.where(band_mask[None], band_score, NEGATIVE)
    summ_score = (
        jnp.einsum("tgd,kd->gtk", group_query, summ_keys, preferred_element_type=jnp.float32)
        * scale
    )
    summ_score = jnp.where(summ_mask[None], summ_score, NEGATIVE)
    highest = jnp.maximum(jnp.max(band_score, -1), jnp.max(summ_score, -1))
    total = jnp.sum(jnp.exp(band_score - highest[..., None]), -1) + jnp.sum(
        jnp.exp(summ_score - highest[..., None]), -1
    )
    log_total = highest + jnp.log(total)
    band_prob = jnp.exp(band_score - log_total[..., None])
    summ_prob = jnp.exp(summ_score - log_total[..., None])
    band_half = band_prob.astype(jnp.bfloat16)
    summ_half = summ_prob.astype(jnp.bfloat16)
    attended = jnp.einsum("gtk,kd->tgd", band_half, band_vals, preferred_element_type=jnp.float32)
    attended = attended + jnp.einsum(
        "gtk,kd->tgd", summ_half, summ_vals, preferred_element_type=jnp.float32
    )
    attended = lax.optimization_barrier(attended.astype(jnp.bfloat16)).astype(jnp.float32)
    delta = jnp.sum(group_cot.astype(jnp.float32) * attended, -1).T
    band_dprob = jnp.einsum("tgd,kd->gtk", group_cot, band_vals, preferred_element_type=jnp.float32)
    summ_dprob = jnp.einsum("tgd,kd->gtk", group_cot, summ_vals, preferred_element_type=jnp.float32)
    band_dscore = (band_prob * (band_dprob - delta[..., None])).astype(jnp.bfloat16)
    summ_dscore = (summ_prob * (summ_dprob - delta[..., None])).astype(jnp.bfloat16)
    query_part = jnp.einsum(
        "gtk,kd->tgd", band_dscore, band_keys, preferred_element_type=jnp.float32
    )
    query_part = (
        query_part
        + jnp.einsum("gtk,kd->tgd", summ_dscore, summ_keys, preferred_element_type=jnp.float32)
    ) * scale
    key_part = (
        jnp.einsum("gtk,tgd->kd", band_dscore, group_query, preferred_element_type=jnp.float32)
        * scale
    )
    value_part = jnp.einsum("gtk,tgd->kd", band_half, group_cot, preferred_element_type=jnp.float32)
    summ_key_part = (
        jnp.einsum("gtk,tgd->kd", summ_dscore, group_query, preferred_element_type=jnp.float32)
        * scale
    )
    summ_value_part = jnp.einsum(
        "gtk,tgd->kd", summ_half, group_cot, preferred_element_type=jnp.float32
    )
    return (query_part, key_part, value_part, summ_key_part, summ_value_part, log_total, delta)


def body(queries, keys, values, cotangent, summary_positions):
    row_count = queries.shape[0]
    key_cols = keys.shape[1]
    kv_heads = key_cols // HEAD
    group = queries.shape[1] // key_cols
    scale = HEAD ** (-0.5)
    reach = BAND_LENGTH // row_count
    device_count = lax.axis_size("ctx")
    shard_index = lax.axis_index("ctx")
    first_row = shard_index * row_count
    per_device = summary_positions.shape[0] // device_count
    earlier_keys, earlier_vals = ([], [])
    for turn in range(reach):
        prev_keys, prev_vals = passed_along((keys, values), "ctx", reach - turn)
        earlier_keys.append(prev_keys)
        earlier_vals.append(prev_vals)
    band_keys = jnp.concatenate(earlier_keys + [keys], 0)
    band_vals = jnp.concatenate(earlier_vals + [values], 0)
    local_rows = (
        lax.dynamic_slice_in_dim(summary_positions, shard_index * per_device, per_device, 0)
        - first_row
    )
    local_keys = jnp.take(keys, local_rows, axis=0)
    local_vals = jnp.take(values, local_rows, axis=0)
    summ_keys, summ_vals = (
        lax.all_gather(local_keys, "ctx", axis=0, tiled=True),
        lax.all_gather(local_vals, "ctx", axis=0, tiled=True),
    )
    query_pos = first_row + jnp.arange(row_count, dtype=jnp.int32)
    band_pos = first_row - BAND_LENGTH + jnp.arange(BAND_LENGTH + row_count, dtype=jnp.int32)
    distance = query_pos[:, None] - band_pos[None, :]
    band_mask = (distance >= 0) & (distance < BAND_LENGTH) & (band_pos[None, :] >= 0)
    summ_mask = summary_positions[None, :] <= query_pos[:, None]
    query_parts, key_parts, value_parts, summ_kparts, summ_vparts, lse_parts, delta_parts = (
        [],
        [],
        [],
        [],
        [],
        [],
        [],
    )
    for head_group in range(kv_heads):
        query_cols = slice(head_group * group * HEAD, (head_group + 1) * group * HEAD)
        head_cols = slice(head_group * HEAD, (head_group + 1) * HEAD)
        group_query = queries[:, query_cols].reshape(row_count, group, HEAD)
        group_cot = cotangent[:, query_cols].reshape(row_count, group, HEAD)
        outcome = group_pass(
            group_query,
            group_cot,
            band_keys[:, head_cols],
            band_vals[:, head_cols],
            summ_keys[:, head_cols],
            summ_vals[:, head_cols],
            band_mask,
            summ_mask,
            scale,
        )
        query_parts.append(outcome[0].reshape(row_count, group * HEAD))
        key_parts.append(outcome[1])
        value_parts.append(outcome[2])
        summ_kparts.append(outcome[3])
        summ_vparts.append(outcome[4])
        lse_parts.append(outcome[5])
        delta_parts.append(outcome[6])
    query_grad = jnp.concatenate(query_parts, 1).astype(jnp.bfloat16)
    band_kgrad = jnp.concatenate(key_parts, 1)
    band_vgrad = jnp.concatenate(value_parts, 1)
    key_grad = band_kgrad[BAND_LENGTH:]
    value_gradient = band_vgrad[BAND_LENGTH:]
    for turn in range(reach):
        lower = turn * row_count
        back_keys, back_vals = (
            passed_along(
                band_kgrad[lower : lower + row_count].astype(jnp.bfloat16), "ctx", turn - reach
            ).astype(jnp.float32),
            passed_along(
                band_vgrad[lower : lower + row_count].astype(jnp.bfloat16), "ctx", turn - reach
            ).astype(jnp.float32),
        )
        key_grad = key_grad + back_keys
        value_gradient = value_gradient + back_vals
    summ_kterm = jnp.concatenate(summ_kparts, 1)
    summ_vterm = jnp.concatenate(summ_vparts, 1)
    share_keys, share_vals = (
        lax.psum_scatter(summ_kterm, "ctx", scatter_dimension=0, tiled=True),
        lax.psum_scatter(summ_vterm, "ctx", scatter_dimension=0, tiled=True),
    )
    key_grad = key_grad.at[local_rows].add(share_keys)
    value_gradient = value_gradient.at[local_rows].add(share_vals)
    return (query_grad, key_grad.astype(jnp.bfloat16), value_gradient.astype(jnp.bfloat16))


def solution(mesh):
    return jax.shard_map(
        body,
        mesh=mesh,
        in_specs=(P("ctx", None), P("ctx", None), P("ctx", None), P("ctx", None), P()),
        out_specs=(P("ctx", None), P("ctx", None), P("ctx", None)),
        check_vma=False,
    )
```

profile of v0, /device:TPU:1, one launch (start us, length us, event | category | flops | bytes accessed | tf_op | source)
XLA Modules:
  0.0 388.8 jit_solution(9783124111173024778)
XLA Ops:
  7.2 4.9 %collective-permute-start.3 = (bf16[256,512]{1,0:T(8,128)(2,1)}, bf16[256,512]{1,0:T(8,128)(2,1)}, u32[]{:S(2)}, u32[]{:S(2)}) collective-permute-start(bf16[256,512]{1,0:T(8,128)(2,1)} %param.8), channel_id=1, source_target_pairs={{0,1},{1,2},{2,3},{3,4},{4,5},{5,6},{6,7},{7,8},{8,9},{9,10},{10,1... | collective-permute-start | bytes 786440 | tf_op jit(solution)/shard_map/ppermute | solution.py:14
  12.2 4.2 %collective-permute-start.2 = (bf16[256,512]{1,0:T(8,128)(2,1)}, bf16[256,512]{1,0:T(8,128)(2,1)}, u32[]{:S(2)}, u32[]{:S(2)}) collective-permute-start(bf16[256,512]{1,0:T(8,128)(2,1)} %param.8), channel_id=1, source_target_pairs={{0,2},{1,3},{2,4},{3,5},{4,6},{5,7},{6,8},{7,9},{8,10},{9,11},{10,... | collective-permute-start | bytes 786440 | tf_op jit(solution)/shard_map/ppermute | solution.py:14
  16.4 3.3 collective-permute-start.6
  19.7 2.7 collective-permute-start.5
  22.4 4.3 %collective-permute-start.4 = (bf16[256,512]{1,0:T(8,128)(2,1)}, bf16[256,512]{1,0:T(8,128)(2,1)}, u32[]{:S(2)}, u32[]{:S(2)}) collective-permute-start(bf16[256,512]{1,0:T(8,128)(2,1)} %param.9), channel_id=1, source_target_pairs={{0,4},{1,5},{2,6},{3,7},{4,8},{5,9},{6,10},{7,11},{8,12},{9,13},{1... | collective-permute-start | bytes 786440 | tf_op jit(solution)/shard_map/ppermute | solution.py:14
  27.5 1.5 gather_fusion.1
  29.0 1.5 gather_fusion
  31.5 41.0 %all-gather = bf16[128,2,512]{2,1,0:T(2,128)(2,1)S(1)} all-gather(bf16[1,2,512]{2,1,0:T(2,128)(2,1)S(1)} %get-tuple-element.28), channel_id=1, replica_groups=mesh['ctx'=128] {'ctx'}, dimensions={0}, use_global_device_ids=true | all-gather | bytes 264192 | tf_op jit(solution)/shard_map/all_gather | solution.py:96
  72.6 1.4 fusion.98
  75.6 1.3 fusion.103
  76.9 1.4 fusion.107
  78.3 1.6 fusion.33
  80.7 33.2 %all-gather.1 = bf16[128,2,512]{2,1,0:T(2,128)(2,1)S(1)} all-gather(bf16[1,2,512]{2,1,0:T(2,128)(2,1)S(1)} %get-tuple-element.27), channel_id=1, replica_groups=mesh['ctx'=128] {'ctx'}, dimensions={0}, use_global_device_ids=true | all-gather | bytes 264192 | tf_op jit(solution)/shard_map/all_gather | solution.py:97
  114.3 1.1 copy.343
  115.4 1.1 copy.349
  116.6 3.0 collective-permute-start.7
  120.6 2.6 collective-permute-start.1
  124.1 4.5 %collective-permute-start = (bf16[256,512]{1,0:T(8,128)(2,1)}, bf16[256,512]{1,0:T(8,128)(2,1)S(1)}, u32[]{:S(2)}, u32[]{:S(2)}) collective-permute-start(bf16[256,512]{1,0:T(8,128)(2,1)} %param.8), channel_id=1, source_target_pairs={{0,4},{1,5},{2,6},{3,7},{4,8},{5,9},{6,10},{7,11},{8,12},{9,13},{1... | collective-permute-start | bytes 786440 | tf_op jit(solution)/shard_map/ppermute | solution.py:14
  130.6 3.3 collective-permute-done
  152.3 1.2 fusion.102
  160.4 1.1 fusion.3
  170.2 1.1 fusion.7
  173.3 1.2 fusion.13
  175.5 1.2 fusion.95
  176.7 1.7 pad_maximum_fusion
  178.3 1.2 fusion.94
  179.6 1.7 pad_maximum_fusion.1
  182.7 1.5 fusion.43
  185.1 2.6 fusion.44
  188.6 1.5 fusion.42
  190.3 2.3 fusion.97
  192.6 1.3 collective-permute-start.8
  193.9 3.5 collective-permute-start.11
  197.4 1.3 collective-permute-start.10
  198.7 1.4 collective-permute-start.9
  201.2 1.4 collective-permute-start.12
  202.7 2.0 pad_maximum_fusion.3
  204.7 1.1 pad_maximum_fusion.2
  206.2 2.7 collective-permute-start.15
  208.9 5.6 %collective-permute-done.11 = bf16[256,512]{0,1:T(8,128)(2,1)} collective-permute-done((bf16[256,512]{0,1:T(8,128)(2,1)}, bf16[256,512]{0,1:T(8,128)(2,1)}, u32[]{:S(2)}, u32[]{:S(2)}) %collective-permute-start.11) | collective-permute-done | bytes 262176 | tf_op jit(solution)/shard_map/ppermute | solution.py:14
  214.5 1.3 collective-permute-start.14
  215.8 1.3 collective-permute-start.13
  217.1 1.5 fusion.75
  218.8 15.7 %collective-permute-done.15 = bf16[256,512]{0,1:T(8,128)(2,1)S(1)} collective-permute-done((bf16[256,512]{0,1:T(8,128)(2,1)}, bf16[256,512]{0,1:T(8,128)(2,1)S(1)}, u32[]{:S(2)}, u32[]{:S(2)}) %collective-permute-start.15) | collective-permute-done | bytes 262176 | tf_op jit(solution)/shard_map/ppermute | solution.py:14
  235.0 1.2 fusion.72
  236.4 140.0 %all-reduce.5.cloned.1.call-done = (f32[256,512]{0,1:T(8,128)}, f32[256,512]{0,1:T(8,128)}) async-done(((f32[256,512]{0,1:T(8,128)}, f32[256,512]{0,1:T(8,128)}), (f32[256,512]{0,1:T(8,128)}, f32[256,512]{0,1:T(8,128)})) %all-reduce.5.cloned.1.call-update) | async-done | bytes 1048592
  376.4 1.1 constant_dynamic-slice_fusion.1
  377.5 1.1 constant_dynamic-slice_fusion
  (181 shorter events, 54.0 us)
Async XLA Ops:
  7.2 369.2 %all-reduce.5.cloned.1.call-start = ((), (), s32[]{:S(2)}) async-start(), calls=%async_computation | async-start | bytes 2097152
  7.2 127.8 %collective-permute-start.3 = (bf16[256,512]{1,0:T(8,128)(2,1)}, bf16[256,512]{1,0:T(8,128)(2,1)}, u32[]{:S(2)}, u32[]{:S(2)}) collective-permute-start(bf16[256,512]{1,0:T(8,128)(2,1)} %param.8), channel_id=1, source_target_pairs={{0,1},{1,2},{2,3},{3,4},{4,5},{5,6},{6,7},{7,8},{8,9},{9,10},{10,1... | collective-permute-start | bytes 786440 | tf_op jit(solution)/shard_map/ppermute | solution.py:14
  12.2 121.8 %collective-permute-start.2 = (bf16[256,512]{1,0:T(8,128)(2,1)}, bf16[256,512]{1,0:T(8,128)(2,1)}, u32[]{:S(2)}, u32[]{:S(2)}) collective-permute-start(bf16[256,512]{1,0:T(8,128)(2,1)} %param.8), channel_id=1, source_target_pairs={{0,2},{1,3},{2,4},{3,5},{4,6},{5,7},{6,8},{7,9},{8,10},{9,11},{10,... | collective-permute-start | bytes 786440 | tf_op jit(solution)/shard_map/ppermute | solution.py:14
  16.4 107.7 %collective-permute-start.6 = (bf16[256,512]{1,0:T(8,128)(2,1)}, bf16[256,512]{1,0:T(8,128)(2,1)}, u32[]{:S(2)}, u32[]{:S(2)}) collective-permute-start(bf16[256,512]{1,0:T(8,128)(2,1)} %param.9), channel_id=1, source_target_pairs={{0,2},{1,3},{2,4},{3,5},{4,6},{5,7},{6,8},{7,9},{8,10},{9,11},{10,... | collective-permute-start | bytes 786440 | tf_op jit(solution)/shard_map/ppermute | solution.py:14
  19.7 100.9 %collective-permute-start.5 = (bf16[256,512]{1,0:T(8,128)(2,1)}, bf16[256,512]{1,0:T(8,128)(2,1)}, u32[]{:S(2)}, u32[]{:S(2)}) collective-permute-start(bf16[256,512]{1,0:T(8,128)(2,1)} %param.9), channel_id=1, source_target_pairs={{0,3},{1,4},{2,5},{3,6},{4,7},{5,8},{6,9},{7,10},{8,11},{9,12},{10... | collective-permute-start | bytes 786440 | tf_op jit(solution)/shard_map/ppermute | solution.py:14
  22.4 94.2 %collective-permute-start.4 = (bf16[256,512]{1,0:T(8,128)(2,1)}, bf16[256,512]{1,0:T(8,128)(2,1)}, u32[]{:S(2)}, u32[]{:S(2)}) collective-permute-start(bf16[256,512]{1,0:T(8,128)(2,1)} %param.9), channel_id=1, source_target_pairs={{0,4},{1,5},{2,6},{3,7},{4,8},{5,9},{6,10},{7,11},{8,12},{9,13},{1... | collective-permute-start | bytes 786440 | tf_op jit(solution)/shard_map/ppermute | solution.py:14
  72.6 4.3 %copy-start.16 = (bf16[256,512]{1,0:T(8,128)(2,1)}, bf16[256,512]{1,0:T(8,128)(2,1)S(1)}, u32[]{:S(2)}) copy-start(bf16[256,512]{1,0:T(8,128)(2,1)S(1)} %reshape.253) | copy-start | bytes 786436
  74.1 2.7 copy-start.6
  74.3 2.6 copy-start.8
  74.4 3.8 copy-start.10
  75.3 4.6 %copy-start.22 = (bf16[256,2048]{1,0:T(8,128)(2,1)S(1)}, bf16[256,2048]{1,0:T(8,128)(2,1)}, u32[]{:S(2)}) copy-start(bf16[256,2048]{1,0:T(8,128)(2,1)} %param.10) | copy-start | bytes 3145732
  114.1 33.8 %copy-start.18 = (bf16[256,512]{1,0:T(8,128)(2,1)}, bf16[256,512]{1,0:T(8,128)(2,1)S(1)}, u32[]{:S(2)}) copy-start(bf16[256,512]{1,0:T(8,128)(2,1)S(1)} %reshape.255) | copy-start | bytes 786436
  116.5 19.4 %copy-start.32 = (bf16[256,512]{1,0:T(8,128)(2,1)S(1)}, bf16[256,512]{1,0:T(8,128)(2,1)}, u32[]{:S(2)}) copy-start(bf16[256,512]{1,0:T(8,128)(2,1)} %param.8) | copy-start | bytes 786436
  116.5 19.4 %copy-start.5 = (pred[256,1280]{0,1:T(8,128)(4,1)S(1)}, pred[256,1280]{0,1:T(8,128)(4,1)}, u32[]{:S(2)}) copy-start(pred[256,1280]{0,1:T(8,128)(4,1)} %fusion.33) | copy-start | bytes 983044
  116.6 19.4 %copy-start.13 = (bf16[256,512]{0,1:T(8,128)(2,1)S(1)}, bf16[256,512]{0,1:T(8,128)(2,1)}, u32[]{:S(2)}) copy-start(bf16[256,512]{0,1:T(8,128)(2,1)} %copy-done.12) | copy-start | bytes 786436
  116.6 13.0 %collective-permute-start.7 = (bf16[256,512]{1,0:T(8,128)(2,1)}, bf16[256,512]{1,0:T(8,128)(2,1)S(1)}, u32[]{:S(2)}, u32[]{:S(2)}) collective-permute-start(bf16[256,512]{1,0:T(8,128)(2,1)} %param.9), channel_id=1, source_target_pairs={{0,1},{1,2},{2,3},{3,4},{4,5},{5,6},{6,7},{7,8},{8,9},{9,10},{10,1... | collective-permute-start | bytes 786440 | tf_op jit(solution)/shard_map/ppermute | solution.py:14
  120.6 13.4 %collective-permute-start.1 = (bf16[256,512]{1,0:T(8,128)(2,1)}, bf16[256,512]{1,0:T(8,128)(2,1)S(1)}, u32[]{:S(2)}, u32[]{:S(2)}) collective-permute-start(bf16[256,512]{1,0:T(8,128)(2,1)} %param.8), channel_id=1, source_target_pairs={{0,3},{1,4},{2,5},{3,6},{4,7},{5,8},{6,9},{7,10},{8,11},{9,12},{10... | collective-permute-start | bytes 786440 | tf_op jit(solution)/shard_map/ppermute | solution.py:14
  124.1 9.8 %collective-permute-start = (bf16[256,512]{1,0:T(8,128)(2,1)}, bf16[256,512]{1,0:T(8,128)(2,1)S(1)}, u32[]{:S(2)}, u32[]{:S(2)}) collective-permute-start(bf16[256,512]{1,0:T(8,128)(2,1)} %param.8), channel_id=1, source_target_pairs={{0,4},{1,5},{2,6},{3,7},{4,8},{5,9},{6,10},{7,11},{8,12},{9,13},{1... | collective-permute-start | bytes 786440 | tf_op jit(solution)/shard_map/ppermute | solution.py:14
  136.0 45.3 %copy-start.14 = (bf16[1280,512]{1,0:T(8,128)(2,1)}, bf16[1280,512]{1,0:T(8,128)(2,1)S(1)}, u32[]{:S(2)}) copy-start(bf16[1280,512]{1,0:T(8,128)(2,1)S(1)} %constant_dynamic-update-slice_fusion) | copy-start | bytes 3932164
  142.4 1.1 copy-start.11
  151.2 1.1 copy-start.9
  152.3 1.2 copy-start.4
  160.4 1.1 copy-start.7
  161.5 11.7 %copy-start = (bf16[4,256,1280]{1,2,0:T(8,128)(2,1)}, bf16[4,256,1280]{1,2,0:T(8,128)(2,1)S(1)}, u32[]{:S(2)}) copy-start(bf16[4,256,1280]{1,2,0:T(8,128)(2,1)S(1)} %fusion.3) | copy-start | bytes 7864324
  161.5 2.0 copy-start.3
  171.3 3.2 copy-start.1
  181.3 1.4 copy-start.20
  184.2 4.4 %copy-start.2 = (bf16[4,256,1280]{1,2,0:T(8,128)(2,1)S(1)}, bf16[4,256,1280]{1,2,0:T(8,128)(2,1)}, u32[]{:S(2)}) copy-start(bf16[4,256,1280]{1,2,0:T(8,128)(2,1)} %copy-done.1) | copy-start | bytes 7864324
  184.2 4.4 %copy-start.21 = (f32[128,4,256]{2,0,1:T(8,128)S(1)}, f32[128,4,256]{2,0,1:T(8,128)}, u32[]{:S(2)}) copy-start(f32[128,4,256]{2,0,1:T(8,128)} %fusion.88) | copy-start | bytes 1572868
  190.1 10.1 %copy-start.15 = (bf16[1280,512]{0,1:T(8,128)(2,1)S(1)}, bf16[1280,512]{0,1:T(8,128)(2,1)}, u32[]{:S(2)}) copy-start(bf16[1280,512]{0,1:T(8,128)(2,1)} %fusion.94) | copy-start | bytes 3932164
  190.1 12.5 %copy-start.26 = (f32[256,128]{0,1:T(8,128)S(1)}, f32[256,128]{0,1:T(8,128)}, u32[]{:S(2)}) copy-start(f32[256,128]{0,1:T(8,128)} %fusion.55) | copy-start | bytes 393220
  190.1 12.5 %copy-start.27 = (f32[256,128]{0,1:T(8,128)S(1)}, f32[256,128]{0,1:T(8,128)}, u32[]{:S(2)}) copy-start(f32[256,128]{0,1:T(8,128)} %fusion.56) | copy-start | bytes 393220
  190.1 12.5 %copy-start.28 = (f32[256,128]{0,1:T(8,128)S(1)}, f32[256,128]{0,1:T(8,128)}, u32[]{:S(2)}) copy-start(f32[256,128]{0,1:T(8,128)} %fusion.54) | copy-start | bytes 393220
  190.1 12.5 %copy-start.29 = (f32[256,128]{0,1:T(8,128)S(1)}, f32[256,128]{0,1:T(8,128)}, u32[]{:S(2)}) copy-start(f32[256,128]{0,1:T(8,128)} %convolution_bitcast_fusion.12) | copy-start | bytes 393220
  190.1 12.5 %copy-start.30 = (f32[256,128]{0,1:T(8,128)S(1)}, f32[256,128]{0,1:T(8,128)}, u32[]{:S(2)}) copy-start(f32[256,128]{0,1:T(8,128)} %convolution_bitcast_fusion.14) | copy-start | bytes 393220
  190.2 12.5 %copy-start.31 = (f32[256,128]{0,1:T(8,128)S(1)}, f32[256,128]{0,1:T(8,128)}, u32[]{:S(2)}) copy-start(f32[256,128]{0,1:T(8,128)} %convolution_bitcast_fusion.13) | copy-start | bytes 393220
  192.6 13.6 %collective-permute-start.8 = (bf16[256,512]{0,1:T(8,128)(2,1)}, bf16[256,512]{0,1:T(8,128)(2,1)}, u32[]{:S(2)}, u32[]{:S(2)}) collective-permute-start(bf16[256,512]{0,1:T(8,128)(2,1)} %get-tuple-element.15), channel_id=1, source_target_pairs={{4,0},{5,1},{6,2},{7,3},{8,4},{9,5},{10,6},{11,7},{12,8},{13,9},{1... | collective-permute-start | bytes 786440 | tf_op jit(solution)/shard_map/ppermute | solution.py:14
  193.9 20.6 %collective-permute-start.11 = (bf16[256,512]{0,1:T(8,128)(2,1)}, bf16[256,512]{0,1:T(8,128)(2,1)}, u32[]{:S(2)}, u32[]{:S(2)}) collective-permute-start(bf16[256,512]{0,1:T(8,128)(2,1)} %get-tuple-element.16), channel_id=1, source_target_pairs={{1,0},{2,1},{3,2},{4,3},{5,4},{6,5},{7,6},{8,7},{9,8},{10,9},{11,1... | collective-permute-start | bytes 786440 | tf_op jit(solution)/shard_map/ppermute | solution.py:14
  197.4 18.4 %collective-permute-start.10 = (bf16[256,512]{0,1:T(8,128)(2,1)}, bf16[256,512]{0,1:T(8,128)(2,1)}, u32[]{:S(2)}, u32[]{:S(2)}) collective-permute-start(bf16[256,512]{0,1:T(8,128)(2,1)} %get-tuple-element.17), channel_id=1, source_target_pairs={{2,0},{3,1},{4,2},{5,3},{6,4},{7,5},{8,6},{9,7},{10,8},{11,9},{12,... | collective-permute-start | bytes 786440 | tf_op jit(solution)/shard_map/ppermute | solution.py:14
  198.7 6.0 %copy-start.23 = (bf16[256,512]{1,0:T(8,128)(2,1)S(1)}, bf16[256,512]{1,0:T(8,128)(2,1)}, u32[]{:S(2)}) copy-start(bf16[256,512]{1,0:T(8,128)(2,1)} %copy.234) | copy-start | bytes 786436
  198.7 6.0 %copy-start.24 = (bf16[256,512]{1,0:T(8,128)(2,1)S(1)}, bf16[256,512]{1,0:T(8,128)(2,1)}, u32[]{:S(2)}) copy-start(bf16[256,512]{1,0:T(8,128)(2,1)} %copy.232) | copy-start | bytes 786436
  198.7 6.0 %copy-start.25 = (bf16[256,512]{1,0:T(8,128)(2,1)S(1)}, bf16[256,512]{1,0:T(8,128)(2,1)}, u32[]{:S(2)}) copy-start(bf16[256,512]{1,0:T(8,128)(2,1)} %copy.233) | copy-start | bytes 786436
  198.7 18.4 %collective-permute-start.9 = (bf16[256,512]{0,1:T(8,128)(2,1)}, bf16[256,512]{0,1:T(8,128)(2,1)}, u32[]{:S(2)}, u32[]{:S(2)}) collective-permute-start(bf16[256,512]{0,1:T(8,128)(2,1)} %get-tuple-element.18), channel_id=1, source_target_pairs={{3,0},{4,1},{5,2},{6,3},{7,4},{8,5},{9,6},{10,7},{11,8},{12,9},{13... | collective-permute-start | bytes 786440 | tf_op jit(solution)/shard_map/ppermute | solution.py:14
  201.2 14.6 %copy-start.33 = (bf16[256,512]{0,1:T(8,128)(2,1)S(1)}, bf16[256,512]{0,1:T(8,128)(2,1)}, u32[]{:S(2)}) copy-start(bf16[256,512]{0,1:T(8,128)(2,1)} %get-tuple-element.14) | copy-start | bytes 786436
  201.2 17.6 %collective-permute-start.12 = (bf16[256,512]{0,1:T(8,128)(2,1)}, bf16[256,512]{0,1:T(8,128)(2,1)S(1)}, u32[]{:S(2)}, u32[]{:S(2)}) collective-permute-start(bf16[256,512]{0,1:T(8,128)(2,1)} %get-tuple-element.11), channel_id=1, source_target_pairs={{4,0},{5,1},{6,2},{7,3},{8,4},{9,5},{10,6},{11,7},{12,8},{13,9},{1... | collective-permute-start | bytes 786440 | tf_op jit(solution)/shard_map/ppermute | solution.py:14
  206.2 28.4 %collective-permute-start.15 = (bf16[256,512]{0,1:T(8,128)(2,1)}, bf16[256,512]{0,1:T(8,128)(2,1)S(1)}, u32[]{:S(2)}, u32[]{:S(2)}) collective-permute-start(bf16[256,512]{0,1:T(8,128)(2,1)} %get-tuple-element.12), channel_id=1, source_target_pairs={{1,0},{2,1},{3,2},{4,3},{5,4},{6,5},{7,6},{8,7},{9,8},{10,9},{11,1... | collective-permute-start | bytes 786440 | tf_op jit(solution)/shard_map/ppermute | solution.py:14
  214.5 20.5 %collective-permute-start.14 = (bf16[256,512]{0,1:T(8,128)(2,1)}, bf16[256,512]{0,1:T(8,128)(2,1)S(1)}, u32[]{:S(2)}, u32[]{:S(2)}) collective-permute-start(bf16[256,512]{0,1:T(8,128)(2,1)} %get-tuple-element.13), channel_id=1, source_target_pairs={{2,0},{3,1},{4,2},{5,3},{6,4},{7,5},{8,6},{9,7},{10,8},{11,9},{12,... | collective-permute-start | bytes 786440 | tf_op jit(solution)/shard_map/ppermute | solution.py:14
  215.8 19.2 %collective-permute-start.13 = (bf16[256,512]{0,1:T(8,128)(2,1)S(1)}, bf16[256,512]{0,1:T(8,128)(2,1)S(1)}, u32[]{:S(2)}, u32[]{:S(2)}) collective-permute-start(bf16[256,512]{0,1:T(8,128)(2,1)S(1)} %copy-done.33), channel_id=1, source_target_pairs={{3,0},{4,1},{5,2},{6,3},{7,4},{8,5},{9,6},{10,7},{11,8},{12,9},{13... | collective-permute-start | bytes 786440 | tf_op jit(solution)/shard_map/ppermute | solution.py:14
  (3 other events, 2.6 us)
Sparse Core Ops, SparseCore 0:
  204.8 171.5 all-reduce.4
where the time goes:
time: 390 us; the launch traced here: 389 us
  waiting for transfers between devices  165 us (42%)
  blocking collectives  74.2 us (19%)
  starting transfers between devices  43.8 us (11%)
  matrix products  43.2 us (11%)
  local copies, waits for them, and re-layouts  25.2 us (6%)
  other arithmetic  21.8 us (6%)
  between operations  15.2 us (4%)
    unnamed x2, waiting for transfers between devices  140 us
    ppermute x16, starting transfers between devices, passed_along(): return lax.ppermute(block, axis, route)  43.7 us
    all_gather x1, blocking collectives, body(): lax.all_gather(local_keys, 'ctx', axis=0, tiled=True)  41 us
    all_gather x1, blocking collectives, body(): lax.all_gather(local_vals, 'ctx', axis=0, tiled=True)  33.2 us
    ppermute x16, waiting for transfers between devices, passed_along(): return lax.ppermute(block, axis, route)  25.5 us
    unnamed x88, local copies, waits for them, and re-layouts  12.2 us
  transfers between devices with their start and end apart: 17, of which 6 were waited for; matrix products, arithmetic and copies ran while one was open for 7% of the time, Pallas kernels for 0%

commit v1 on v0

--- a/solution.py
+++ b/solution.py
@@ -93,7 +93,9 @@
     local_keys = jnp.take(keys, local_rows, axis=0)
     local_vals = jnp.take(values, local_rows, axis=0)
     summ_keys, summ_vals = (
-        lax.all_gather(local_keys, "ctx", axis=0, tiled=True),
+        jnp.concatenate(
+            lax.all_to_all(jnp.stack([local_keys] * lax.axis_size("ctx")), "ctx", 0, 0), axis=0
+        ),
         lax.all_gather(local_vals, "ctx", axis=0, tiled=True),
     )
     query_pos = first_row + jnp.arange(row_count, dtype=jnp.int32)

time: 390 us -> 355 us (0.910)
  blocking collectives: 74.2 us -> 37 us
  starting transfers between devices: 43.8 us -> 50 us
    all_gather x1 -> x0, blocking collectives: 41 us -> none  [body(): lax.all_gather(local_keys, 'ctx', axis=0, tiled=True)]
    all_to_all x0 -> x1, starting transfers between devices: none -> 7.09 us  [body(): lax.all_to_all(jnp.stack([local_keys] * lax.axis_size('ctx')), 'ctx', 0, 0)]
    unnamed x88 -> x91, local copies, waits for them, and re-layouts: 12.2 us -> 9.81 us
  transfers between devices with their start and end apart: 17 -> 18, of which waited for: 6 -> 5; matrix products, arithmetic and copies ran while one was open for 7% -> 7% of each run, Pallas kernels for 0% -> 0%
where the time goes in v1:
time: 355 us; the launch traced here: 354 us
  waiting for transfers between devices  167 us (47%)
  starting transfers between devices  50 us (14%)
  matrix products  41.2 us (12%)
  blocking collectives  37 us (10%)
  local copies, waits for them, and re-layouts  23.3 us (7%)
  other arithmetic  20.4 us (6%)
  between operations  15.3 us (4%)
    unnamed x2, waiting for transfers between devices  140 us
    ppermute x16, starting transfers between devices, passed_along(): return lax.ppermute(block, axis, route)  42.8 us
    all_gather x1, blocking collectives, body(): lax.all_gather(local_vals, 'ctx', axis=0, tiled=True)  37 us
    ppermute x16, waiting for transfers between devices, passed_along(): return lax.ppermute(block, axis, route)  27.1 us
    unnamed x91, local copies, waits for them, and re-layouts  9.81 us
  transfers between devices with their start and end apart: 18, of which 5 were waited for; matrix products, arithmetic and copies ran while one was open for 7% of the time, Pallas kernels for 0%

profile of v1, /device:TPU:1, one launch (start us, length us, event | category | flops | bytes accessed | tf_op | source)
XLA Modules:
  0.0 353.9 jit_solution(10718391613768321283)
XLA Ops:
  7.2 5.1 %collective-permute-start.3 = (bf16[256,512]{1,0:T(8,128)(2,1)}, bf16[256,512]{1,0:T(8,128)(2,1)}, u32[]{:S(2)}, u32[]{:S(2)}) collective-permute-start(bf16[256,512]{1,0:T(8,128)(2,1)} %param.8), channel_id=1, source_target_pairs={{0,1},{1,2},{2,3},{3,4},{4,5},{5,6},{6,7},{7,8},{8,9},{9,10},{10,1... | collective-permute-start | bytes 786440 | tf_op jit(solution)/shard_map/ppermute | solution.py:14
  12.3 4.2 %collective-permute-start.2 = (bf16[256,512]{1,0:T(8,128)(2,1)}, bf16[256,512]{1,0:T(8,128)(2,1)}, u32[]{:S(2)}, u32[]{:S(2)}) collective-permute-start(bf16[256,512]{1,0:T(8,128)(2,1)} %param.8), channel_id=1, source_target_pairs={{0,2},{1,3},{2,4},{3,5},{4,6},{5,7},{6,8},{7,9},{8,10},{9,11},{10,... | collective-permute-start | bytes 786440 | tf_op jit(solution)/shard_map/ppermute | solution.py:14
  16.5 3.3 collective-permute-start.6
  19.8 2.8 collective-permute-start.5
  22.5 4.3 %collective-permute-start.4 = (bf16[256,512]{1,0:T(8,128)(2,1)}, bf16[256,512]{1,0:T(8,128)(2,1)}, u32[]{:S(2)}, u32[]{:S(2)}) collective-permute-start(bf16[256,512]{1,0:T(8,128)(2,1)} %param.9), channel_id=1, source_target_pairs={{0,4},{1,5},{2,6},{3,7},{4,8},{5,9},{6,10},{7,11},{8,12},{9,13},{1... | collective-permute-start | bytes 786440 | tf_op jit(solution)/shard_map/ppermute | solution.py:14
  27.6 1.5 gather_fusion.1
  29.1 1.5 gather_fusion
  31.6 7.1 %all-to-all-start = ((bf16[128,2,512]{2,1,0:T(2,128)(2,1)}), bf16[128,2,512]{2,1,0:T(2,128)(2,1)S(1)}, u32[]{:S(2)}, u32[]{:S(2)}) async-start(bf16[128,2,512]{2,1,0:T(2,128)(2,1)} %stack.2), calls=%async_computation | async-start | bytes 524288 | tf_op jit(solution)/shard_map/all_to_all | solution.py:97
  38.8 2.0 fusion.97
  42.5 37.0 %all-gather = bf16[128,2,512]{2,1,0:T(2,128)(2,1)S(1)} all-gather(bf16[1,2,512]{2,1,0:T(2,128)(2,1)S(1)} %get-tuple-element.27), channel_id=1, replica_groups=mesh['ctx'=128] {'ctx'}, dimensions={0}, use_global_device_ids=true | all-gather | bytes 264192 | tf_op jit(solution)/shard_map/all_gather | solution.py:99
  79.6 1.2 copy.339
  83.4 2.9 collective-permute-start.7
  87.3 3.5 collective-permute-start.1
  91.8 3.5 %collective-permute-start = (bf16[256,512]{1,0:T(8,128)(2,1)S(1)}, bf16[256,512]{1,0:T(8,128)(2,1)S(1)}, u32[]{:S(2)}, u32[]{:S(2)}) collective-permute-start(bf16[256,512]{1,0:T(8,128)(2,1)S(1)} %copy-done.33), channel_id=1, source_target_pairs={{0,4},{1,5},{2,6},{3,7},{4,8},{5,9},{6,10},{7,11},{8,12},{9,13},{1... | collective-permute-start | bytes 786440 | tf_op jit(solution)/shard_map/ppermute | solution.py:14
  96.4 5.7 %collective-permute-done = bf16[256,512]{1,0:T(8,128)(2,1)S(1)} collective-permute-done((bf16[256,512]{1,0:T(8,128)(2,1)S(1)}, bf16[256,512]{1,0:T(8,128)(2,1)S(1)}, u32[]{:S(2)}, u32[]{:S(2)}) %collective-permute-start) | collective-permute-done | bytes 262176 | tf_op jit(solution)/shard_map/ppermute | solution.py:14
  110.4 1.1 fusion.1
  117.1 1.1 fusion.89
  119.2 1.1 fusion.5
  120.3 1.2 fusion.101
  128.5 1.1 fusion.3
  135.1 1.1 fusion.88
  137.2 1.1 fusion.7
  140.5 1.2 fusion.13
  142.6 1.2 fusion.94
  143.8 1.7 pad_maximum_fusion
  145.5 1.2 fusion.93
  146.7 1.7 pad_maximum_fusion.1
  149.8 1.5 fusion.43
  152.2 2.7 fusion.44
  155.7 1.5 fusion.42
  157.4 2.3 fusion.96
  159.8 1.3 collective-permute-start.8
  161.1 2.6 collective-permute-start.11
  163.7 1.3 collective-permute-start.10
  165.0 1.4 collective-permute-start.9
  167.5 1.4 collective-permute-start.12
  169.0 2.0 pad_maximum_fusion.3
  171.0 1.1 pad_maximum_fusion.2
  172.1 2.7 collective-permute-start.15
  174.9 4.1 %collective-permute-done.11 = bf16[256,512]{0,1:T(8,128)(2,1)} collective-permute-done((bf16[256,512]{0,1:T(8,128)(2,1)}, bf16[256,512]{0,1:T(8,128)(2,1)}, u32[]{:S(2)}, u32[]{:S(2)}) %collective-permute-start.11) | collective-permute-done | bytes 262176 | tf_op jit(solution)/shard_map/ppermute | solution.py:14
  179.0 1.3 collective-permute-start.14
  180.3 1.3 collective-permute-start.13
  181.6 1.5 fusion.75
  183.3 16.7 %collective-permute-done.15 = bf16[256,512]{0,1:T(8,128)(2,1)S(1)} collective-permute-done((bf16[256,512]{0,1:T(8,128)(2,1)}, bf16[256,512]{0,1:T(8,128)(2,1)S(1)}, u32[]{:S(2)}, u32[]{:S(2)}) %collective-permute-start.15) | collective-permute-done | bytes 262176 | tf_op jit(solution)/shard_map/ppermute | solution.py:14
  200.5 1.2 fusion.72
  201.9 139.6 %all-reduce.5.cloned.1.call-done = (f32[256,512]{0,1:T(8,128)}, f32[256,512]{0,1:T(8,128)}) async-done(((f32[256,512]{0,1:T(8,128)}, f32[256,512]{0,1:T(8,128)}), (f32[256,512]{0,1:T(8,128)}, f32[256,512]{0,1:T(8,128)})) %all-reduce.5.cloned.1.call-update) | async-done | bytes 1048592
  341.5 1.1 constant_dynamic-slice_fusion.1
  342.5 1.1 constant_dynamic-slice_fusion
  (187 shorter events, 48.8 us)
Async XLA Ops:
  7.2 33.6 %copy-start.21 = (bf16[256,2048]{1,0:T(8,128)(2,1)S(1)}, bf16[256,2048]{1,0:T(8,128)(2,1)}, u32[]{:S(2)}) copy-start(bf16[256,2048]{1,0:T(8,128)(2,1)} %param.10) | copy-start | bytes 3145732
  7.2 96.0 %collective-permute-start.3 = (bf16[256,512]{1,0:T(8,128)(2,1)}, bf16[256,512]{1,0:T(8,128)(2,1)}, u32[]{:S(2)}, u32[]{:S(2)}) collective-permute-start(bf16[256,512]{1,0:T(8,128)(2,1)} %param.8), channel_id=1, source_target_pairs={{0,1},{1,2},{2,3},{3,4},{4,5},{5,6},{6,7},{7,8},{8,9},{9,10},{10,1... | collective-permute-start | bytes 786440 | tf_op jit(solution)/shard_map/ppermute | solution.py:14
  12.3 89.9 %collective-permute-start.2 = (bf16[256,512]{1,0:T(8,128)(2,1)}, bf16[256,512]{1,0:T(8,128)(2,1)}, u32[]{:S(2)}, u32[]{:S(2)}) collective-permute-start(bf16[256,512]{1,0:T(8,128)(2,1)} %param.8), channel_id=1, source_target_pairs={{0,2},{1,3},{2,4},{3,5},{4,6},{5,7},{6,8},{7,9},{8,10},{9,11},{10,... | collective-permute-start | bytes 786440 | tf_op jit(solution)/shard_map/ppermute | solution.py:14
  16.5 75.3 %collective-permute-start.6 = (bf16[256,512]{1,0:T(8,128)(2,1)}, bf16[256,512]{1,0:T(8,128)(2,1)}, u32[]{:S(2)}, u32[]{:S(2)}) collective-permute-start(bf16[256,512]{1,0:T(8,128)(2,1)} %param.9), channel_id=1, source_target_pairs={{0,2},{1,3},{2,4},{3,5},{4,6},{5,7},{6,8},{7,9},{8,10},{9,11},{10,... | collective-permute-start | bytes 786440 | tf_op jit(solution)/shard_map/ppermute | solution.py:14
  19.8 67.5 %collective-permute-start.5 = (bf16[256,512]{1,0:T(8,128)(2,1)}, bf16[256,512]{1,0:T(8,128)(2,1)}, u32[]{:S(2)}, u32[]{:S(2)}) collective-permute-start(bf16[256,512]{1,0:T(8,128)(2,1)} %param.9), channel_id=1, source_target_pairs={{0,3},{1,4},{2,5},{3,6},{4,7},{5,8},{6,9},{7,10},{8,11},{9,12},{10... | collective-permute-start | bytes 786440 | tf_op jit(solution)/shard_map/ppermute | solution.py:14
  22.5 60.9 %collective-permute-start.4 = (bf16[256,512]{1,0:T(8,128)(2,1)}, bf16[256,512]{1,0:T(8,128)(2,1)}, u32[]{:S(2)}, u32[]{:S(2)}) collective-permute-start(bf16[256,512]{1,0:T(8,128)(2,1)} %param.9), channel_id=1, source_target_pairs={{0,4},{1,5},{2,6},{3,7},{4,8},{5,9},{6,10},{7,11},{8,12},{9,13},{1... | collective-permute-start | bytes 786440 | tf_op jit(solution)/shard_map/ppermute | solution.py:14
  31.6 50.4 %all-to-all-start = ((bf16[128,2,512]{2,1,0:T(2,128)(2,1)}), bf16[128,2,512]{2,1,0:T(2,128)(2,1)S(1)}, u32[]{:S(2)}, u32[]{:S(2)}) async-start(bf16[128,2,512]{2,1,0:T(2,128)(2,1)} %stack.2), calls=%async_computation | async-start | bytes 524288 | tf_op jit(solution)/shard_map/all_to_all | solution.py:97
  38.7 302.8 %all-reduce.5.cloned.1.call-start = ((), (), s32[]{:S(2)}) async-start(), calls=%async_computation.1 | async-start | bytes 2097152
  41.6 40.3 %copy-start.35 = (s32[256]{0:T(256)S(1)}, s32[256]{0:T(256)}, u32[]{:S(2)}) copy-start(s32[256]{0:T(256)} %param.11) | copy-start | bytes 3076
  42.5 69.0 %copy-start.3 = (pred[256,1280]{0,1:T(8,128)(4,1)}, pred[256,1280]{0,1:T(8,128)(4,1)S(1)}, u32[]{:S(2)}) copy-start(pred[256,1280]{0,1:T(8,128)(4,1)S(1)} %fusion.33) | copy-start | bytes 983044
  79.6 36.2 %copy-start.17 = (bf16[256,512]{1,0:T(8,128)(2,1)}, bf16[256,512]{1,0:T(8,128)(2,1)S(1)}, u32[]{:S(2)}) copy-start(bf16[256,512]{1,0:T(8,128)(2,1)S(1)} %reshape.259) | copy-start | bytes 786436
  79.6 1.9 copy-start.25
  80.8 2.3 copy-start.5
  81.0 1.8 copy-start.7
  81.1 35.0 %copy-start.9 = (bf16[256,512]{0,1:T(8,128)(2,1)}, bf16[256,512]{0,1:T(8,128)(2,1)S(1)}, u32[]{:S(2)}) copy-start(bf16[256,512]{0,1:T(8,128)(2,1)S(1)} %copy.342) | copy-start | bytes 786436
  81.3 27.5 %copy-start.11 = (bf16[256,512]{0,1:T(8,128)(2,1)}, bf16[256,512]{0,1:T(8,128)(2,1)S(1)}, u32[]{:S(2)}) copy-start(bf16[256,512]{0,1:T(8,128)(2,1)S(1)} %copy.348) | copy-start | bytes 786436
  82.1 35.0 %copy-start.15 = (bf16[256,512]{1,0:T(8,128)(2,1)}, bf16[256,512]{1,0:T(8,128)(2,1)S(1)}, u32[]{:S(2)}) copy-start(bf16[256,512]{1,0:T(8,128)(2,1)S(1)} %reshape.210) | copy-start | bytes 786436
  82.1 1.3 copy-start.32
  82.5 4.8 %copy-start.33 = (bf16[256,512]{1,0:T(8,128)(2,1)S(1)}, bf16[256,512]{1,0:T(8,128)(2,1)}, u32[]{:S(2)}) copy-start(bf16[256,512]{1,0:T(8,128)(2,1)} %param.8) | copy-start | bytes 786436
  83.4 12.9 %collective-permute-start.7 = (bf16[256,512]{1,0:T(8,128)(2,1)S(1)}, bf16[256,512]{1,0:T(8,128)(2,1)S(1)}, u32[]{:S(2)}, u32[]{:S(2)}) collective-permute-start(bf16[256,512]{1,0:T(8,128)(2,1)S(1)} %copy-done.32), channel_id=1, source_target_pairs={{0,1},{1,2},{2,3},{3,4},{4,5},{5,6},{6,7},{7,8},{8,9},{9,10},{10,1... | collective-permute-start | bytes 786440 | tf_op jit(solution)/shard_map/ppermute | solution.py:14
  87.3 14.8 %collective-permute-start.1 = (bf16[256,512]{1,0:T(8,128)(2,1)S(1)}, bf16[256,512]{1,0:T(8,128)(2,1)S(1)}, u32[]{:S(2)}, u32[]{:S(2)}) collective-permute-start(bf16[256,512]{1,0:T(8,128)(2,1)S(1)} %copy-done.33), channel_id=1, source_target_pairs={{0,3},{1,4},{2,5},{3,6},{4,7},{5,8},{6,9},{7,10},{8,11},{9,12},{10... | collective-permute-start | bytes 786440 | tf_op jit(solution)/shard_map/ppermute | solution.py:14
  91.8 10.3 %collective-permute-start = (bf16[256,512]{1,0:T(8,128)(2,1)S(1)}, bf16[256,512]{1,0:T(8,128)(2,1)S(1)}, u32[]{:S(2)}, u32[]{:S(2)}) collective-permute-start(bf16[256,512]{1,0:T(8,128)(2,1)S(1)} %copy-done.33), channel_id=1, source_target_pairs={{0,4},{1,5},{2,6},{3,7},{4,8},{5,9},{6,10},{7,11},{8,12},{9,13},{1... | collective-permute-start | bytes 786440 | tf_op jit(solution)/shard_map/ppermute | solution.py:14
  104.2 44.2 %copy-start.13 = (bf16[1280,512]{1,0:T(8,128)(2,1)}, bf16[1280,512]{1,0:T(8,128)(2,1)S(1)}, u32[]{:S(2)}) copy-start(bf16[1280,512]{1,0:T(8,128)(2,1)S(1)} %constant_dynamic-update-slice_fusion) | copy-start | bytes 3932164
  125.0 1.4 copy-start.16
  129.5 10.9 %copy-start = (bf16[4,256,1280]{1,2,0:T(8,128)(2,1)}, bf16[4,256,1280]{1,2,0:T(8,128)(2,1)S(1)}, u32[]{:S(2)}) copy-start(bf16[4,256,1280]{1,2,0:T(8,128)(2,1)S(1)} %fusion.3) | copy-start | bytes 7864324
  138.3 3.3 copy-start.1
  148.4 1.4 copy-start.19
  151.3 4.4 %copy-start.2 = (bf16[4,256,1280]{1,2,0:T(8,128)(2,1)S(1)}, bf16[4,256,1280]{1,2,0:T(8,128)(2,1)}, u32[]{:S(2)}) copy-start(bf16[4,256,1280]{1,2,0:T(8,128)(2,1)} %copy-done.1) | copy-start | bytes 7864324
  151.3 4.4 %copy-start.20 = (f32[128,4,256]{2,0,1:T(8,128)S(1)}, f32[128,4,256]{2,0,1:T(8,128)}, u32[]{:S(2)}) copy-start(f32[128,4,256]{2,0,1:T(8,128)} %fusion.88) | copy-start | bytes 1572868
  157.2 9.2 %copy-start.14 = (bf16[1280,512]{0,1:T(8,128)(2,1)S(1)}, bf16[1280,512]{0,1:T(8,128)(2,1)}, u32[]{:S(2)}) copy-start(bf16[1280,512]{0,1:T(8,128)(2,1)} %fusion.93) | copy-start | bytes 3932164
  157.2 11.7 %copy-start.26 = (f32[256,128]{0,1:T(8,128)S(1)}, f32[256,128]{0,1:T(8,128)}, u32[]{:S(2)}) copy-start(f32[256,128]{0,1:T(8,128)} %fusion.55) | copy-start | bytes 393220
  157.2 11.7 %copy-start.27 = (f32[256,128]{0,1:T(8,128)S(1)}, f32[256,128]{0,1:T(8,128)}, u32[]{:S(2)}) copy-start(f32[256,128]{0,1:T(8,128)} %fusion.56) | copy-start | bytes 393220
  157.3 11.7 %copy-start.28 = (f32[256,128]{0,1:T(8,128)S(1)}, f32[256,128]{0,1:T(8,128)}, u32[]{:S(2)}) copy-start(f32[256,128]{0,1:T(8,128)} %fusion.54) | copy-start | bytes 393220
  157.3 11.7 %copy-start.29 = (f32[256,128]{0,1:T(8,128)S(1)}, f32[256,128]{0,1:T(8,128)}, u32[]{:S(2)}) copy-start(f32[256,128]{0,1:T(8,128)} %convolution_bitcast_fusion.12) | copy-start | bytes 393220
  157.3 11.7 %copy-start.30 = (f32[256,128]{0,1:T(8,128)S(1)}, f32[256,128]{0,1:T(8,128)}, u32[]{:S(2)}) copy-start(f32[256,128]{0,1:T(8,128)} %convolution_bitcast_fusion.14) | copy-start | bytes 393220
  157.3 11.7 %copy-start.31 = (f32[256,128]{0,1:T(8,128)S(1)}, f32[256,128]{0,1:T(8,128)}, u32[]{:S(2)}) copy-start(f32[256,128]{0,1:T(8,128)} %convolution_bitcast_fusion.13) | copy-start | bytes 393220
  159.8 12.3 %collective-permute-start.8 = (bf16[256,512]{0,1:T(8,128)(2,1)}, bf16[256,512]{0,1:T(8,128)(2,1)}, u32[]{:S(2)}, u32[]{:S(2)}) collective-permute-start(bf16[256,512]{0,1:T(8,128)(2,1)} %get-tuple-element.15), channel_id=1, source_target_pairs={{4,0},{5,1},{6,2},{7,3},{8,4},{9,5},{10,6},{11,7},{12,8},{13,9},{1... | collective-permute-start | bytes 786440 | tf_op jit(solution)/shard_map/ppermute | solution.py:14
  161.1 17.9 %collective-permute-start.11 = (bf16[256,512]{0,1:T(8,128)(2,1)}, bf16[256,512]{0,1:T(8,128)(2,1)}, u32[]{:S(2)}, u32[]{:S(2)}) collective-permute-start(bf16[256,512]{0,1:T(8,128)(2,1)} %get-tuple-element.16), channel_id=1, source_target_pairs={{1,0},{2,1},{3,2},{4,3},{5,4},{6,5},{7,6},{8,7},{9,8},{10,9},{11,1... | collective-permute-start | bytes 786440 | tf_op jit(solution)/shard_map/ppermute | solution.py:14
  163.7 16.6 %collective-permute-start.10 = (bf16[256,512]{0,1:T(8,128)(2,1)}, bf16[256,512]{0,1:T(8,128)(2,1)}, u32[]{:S(2)}, u32[]{:S(2)}) collective-permute-start(bf16[256,512]{0,1:T(8,128)(2,1)} %get-tuple-element.17), channel_id=1, source_target_pairs={{2,0},{3,1},{4,2},{5,3},{6,4},{7,5},{8,6},{9,7},{10,8},{11,9},{12,... | collective-permute-start | bytes 786440 | tf_op jit(solution)/shard_map/ppermute | solution.py:14
  165.0 6.0 %copy-start.22 = (bf16[256,512]{1,0:T(8,128)(2,1)S(1)}, bf16[256,512]{1,0:T(8,128)(2,1)}, u32[]{:S(2)}) copy-start(bf16[256,512]{1,0:T(8,128)(2,1)} %copy.234) | copy-start | bytes 786436
  165.0 6.0 %copy-start.23 = (bf16[256,512]{1,0:T(8,128)(2,1)S(1)}, bf16[256,512]{1,0:T(8,128)(2,1)}, u32[]{:S(2)}) copy-start(bf16[256,512]{1,0:T(8,128)(2,1)} %copy.232) | copy-start | bytes 786436
  165.0 6.0 %copy-start.24 = (bf16[256,512]{1,0:T(8,128)(2,1)S(1)}, bf16[256,512]{1,0:T(8,128)(2,1)}, u32[]{:S(2)}) copy-start(bf16[256,512]{1,0:T(8,128)(2,1)} %copy.233) | copy-start | bytes 786436
  165.0 16.6 %collective-permute-start.9 = (bf16[256,512]{0,1:T(8,128)(2,1)}, bf16[256,512]{0,1:T(8,128)(2,1)}, u32[]{:S(2)}, u32[]{:S(2)}) collective-permute-start(bf16[256,512]{0,1:T(8,128)(2,1)} %get-tuple-element.18), channel_id=1, source_target_pairs={{3,0},{4,1},{5,2},{6,3},{7,4},{8,5},{9,6},{10,7},{11,8},{12,9},{13... | collective-permute-start | bytes 786440 | tf_op jit(solution)/shard_map/ppermute | solution.py:14
  167.5 12.8 %copy-start.34 = (bf16[256,512]{0,1:T(8,128)(2,1)S(1)}, bf16[256,512]{0,1:T(8,128)(2,1)}, u32[]{:S(2)}) copy-start(bf16[256,512]{0,1:T(8,128)(2,1)} %get-tuple-element.14) | copy-start | bytes 786436
  167.5 15.8 %collective-permute-start.12 = (bf16[256,512]{0,1:T(8,128)(2,1)}, bf16[256,512]{0,1:T(8,128)(2,1)S(1)}, u32[]{:S(2)}, u32[]{:S(2)}) collective-permute-start(bf16[256,512]{0,1:T(8,128)(2,1)} %get-tuple-element.11), channel_id=1, source_target_pairs={{4,0},{5,1},{6,2},{7,3},{8,4},{9,5},{10,6},{11,7},{12,8},{13,9},{1... | collective-permute-start | bytes 786440 | tf_op jit(solution)/shard_map/ppermute | solution.py:14
  172.1 27.9 %collective-permute-start.15 = (bf16[256,512]{0,1:T(8,128)(2,1)}, bf16[256,512]{0,1:T(8,128)(2,1)S(1)}, u32[]{:S(2)}, u32[]{:S(2)}) collective-permute-start(bf16[256,512]{0,1:T(8,128)(2,1)} %get-tuple-element.12), channel_id=1, source_target_pairs={{1,0},{2,1},{3,2},{4,3},{5,4},{6,5},{7,6},{8,7},{9,8},{10,9},{11,1... | collective-permute-start | bytes 786440 | tf_op jit(solution)/shard_map/ppermute | solution.py:14
  179.0 21.5 %collective-permute-start.14 = (bf16[256,512]{0,1:T(8,128)(2,1)}, bf16[256,512]{0,1:T(8,128)(2,1)S(1)}, u32[]{:S(2)}, u32[]{:S(2)}) collective-permute-start(bf16[256,512]{0,1:T(8,128)(2,1)} %get-tuple-element.13), channel_id=1, source_target_pairs={{2,0},{3,1},{4,2},{5,3},{6,4},{7,5},{8,6},{9,7},{10,8},{11,9},{12,... | collective-permute-start | bytes 786440 | tf_op jit(solution)/shard_map/ppermute | solution.py:14
  180.3 20.2 %collective-permute-start.13 = (bf16[256,512]{0,1:T(8,128)(2,1)S(1)}, bf16[256,512]{0,1:T(8,128)(2,1)S(1)}, u32[]{:S(2)}, u32[]{:S(2)}) collective-permute-start(bf16[256,512]{0,1:T(8,128)(2,1)S(1)} %copy-done.34), channel_id=1, source_target_pairs={{3,0},{4,1},{5,2},{6,3},{7,4},{8,5},{9,6},{10,7},{11,8},{12,9},{13... | collective-permute-start | bytes 786440 | tf_op jit(solution)/shard_map/ppermute | solution.py:14
  (6 other events, 6.4 us)
Sparse Core Ops, SparseCore 0:
  171.1 170.3 all-reduce.4
